TPU v7x, 128 devices: a whole 4x4x4 slice. The times are simulated.
128 devices in a mesh: dp: 16 (over x, y), tensor: 8 (over z, core).
Axes of the slice: x: 4, y: 4, z: 4, core: 2. Of those that a mesh axis runs over, the one named last changes fastest.
Arguments:
- hidden_rows: bfloat16 [256, 32, 8192], P('tensor', 'dp'), may hold values from -6 to 6
- norm_gain: float32 [8192], replicated, may hold values from 0.1 to 1.9
- w_query: bfloat16 [8192, 4096], P(None, 'tensor'), may hold values from -0.0625 to 0.0625
- w_key: bfloat16 [8192, 1024], P(None, 'tensor'), may hold values from -0.0625 to 0.0625
- w_value: bfloat16 [8192, 1024], P(None, 'tensor'), may hold values from -0.0625 to 0.0625
- w_out: bfloat16 [4096, 8192], P('tensor'), may hold values from -1.5 to 1.5
- cache_keys: bfloat16 [32, 2048, 1024], P('dp', None, 'tensor'), may hold values from -6 to 6
- cache_values: bfloat16 [32, 2048, 1024], P('dp', None, 'tensor'), may hold values from -6 to 6
- slot_of_request: int32 [32], replicated, may hold values from 0 to 31, as said below
- span_length: int32 [32], replicated, may hold values from 1 to 256, as said below
- prefix_length: int32 [32], replicated, may hold values from 1 to 2048, as said below
Outputs:
- attention_out: bfloat16 [256, 32, 8192], P('tensor', 'dp')
Inputs may be any that keep to these rules, and one draw needn't show every extreme that they name: `slot_of_request`: a permutation of the slots 0 to 31; slot i lies on dp index i // 2, request r starts on dp index r // 2; there are 2 distinct numbers m, one of them 1, the same for every dp index, such that the 2 requests of dp index i have their slots on the dp indices i XOR m, one on each. `span_length`: some request uses all 256 new positions. `prefix_length`: some request has all 2048 cached positions.
All inputs are finite; a program needn't handle non-finite values.
Results may differ from a plain program's by a relative error of at most 0.019.
Values may be sent and summed in bfloat16 or wider, within the bound.
A program may use at most 128 MiB of HBM per device.

v0:
```python
import jax
import jax.numpy as jnp
from jax import lax
from jax.sharding import PartitionSpec as P

HD = 128
rope_base = 500000.0
norm_eps = 1e-05
masked = -1e30


def rotate(values, position):
    head_width = values.shape[-1]
    half_width = head_width // 2
    frequency = rope_base ** (-(jnp.arange(half_width, dtype=jnp.float32) * 2.0 / head_width))
    angles = position[..., None, None] * frequency
    cosine = jnp.cos(angles)
    sine_part = jnp.sin(angles)
    front_half = values[..., :half_width]
    back_half = values[..., half_width:]
    return jnp.concatenate(
        [front_half * cosine - back_half * sine_part, back_half * cosine + front_half * sine_part],
        axis=-1,
    )


def normalize(hidden_rows, norm_gain):
    floats = hidden_rows.astype(jnp.float32)
    return (
        floats * lax.rsqrt(jnp.mean(floats * floats, axis=-1, keepdims=True) + norm_eps) * norm_gain
    ).astype(jnp.bfloat16)


def project_group(normed, prefix_here, w_query, w_key, w_value):
    piece_rows = lax.all_gather(normed, "tensor", axis=0, tiled=True)
    row_count = piece_rows.shape[0]
    request_count = piece_rows.shape[1]
    positions = (prefix_here[None, :] + jnp.arange(row_count, dtype=jnp.int32)[:, None]).astype(
        jnp.float32
    )
    queries = jnp.einsum("nsd,df->nsf", piece_rows, w_query, preferred_element_type=jnp.float32)
    queries = rotate(queries.reshape(row_count, request_count, -1, HD), positions)
    keys_new = jnp.einsum("nsd,df->nsf", piece_rows, w_key, preferred_element_type=jnp.float32)
    keys_new = rotate(keys_new.reshape(row_count, request_count, -1, HD), positions)
    values_new = jnp.einsum("nsd,df->nsf", piece_rows, w_value, preferred_element_type=jnp.float32)
    return jnp.concatenate(
        [
            queries.reshape(row_count, request_count, -1).astype(jnp.bfloat16),
            keys_new.reshape(row_count, request_count, -1).astype(jnp.bfloat16),
            values_new.astype(jnp.bfloat16),
        ],
        axis=-1,
    )


def attend_slots(packed, cache_keys, cache_values, slot_prefix, slot_length, q_width, kv_width):
    span_rows = packed.shape[0]
    slot_count = packed.shape[1]
    kv_heads = kv_width // HD
    groups = q_width // kv_width
    prefix = cache_keys.shape[1]
    score_scale = HD ** (-0.5)
    queries = packed[..., :q_width].reshape(span_rows, slot_count, kv_heads, groups, HD)
    keys_new = packed[..., q_width : q_width + kv_width].reshape(
        span_rows, slot_count, kv_heads, HD
    )
    values_new = packed[..., q_width + kv_width :].reshape(span_rows, slot_count, kv_heads, HD)
    keys_old = cache_keys.reshape(slot_count, prefix, kv_heads, HD)
    values_old = cache_values.reshape(slot_count, prefix, kv_heads, HD)
    score_old = (
        jnp.einsum("csgmd,spgd->sgmcp", queries, keys_old, preferred_element_type=jnp.float32)
        * score_scale
    )
    score_new = (
        jnp.einsum("csgmd,jsgd->sgmcj", queries, keys_new, preferred_element_type=jnp.float32)
        * score_scale
    )
    keep_old = jnp.arange(prefix, dtype=jnp.int32)[None, :] < slot_prefix[:, None]
    row_index = jnp.arange(span_rows, dtype=jnp.int32)
    keep_new = (row_index[None, None, :] < slot_length[:, None, None]) & (
        row_index[None, None, :] <= row_index[None, :, None]
    )
    score_old = jnp.where(keep_old[:, None, None, None, :], score_old, masked)
    score_new = jnp.where(keep_new[:, None, None, :, :], score_new, masked)
    exp_old = jnp.exp(score_old)
    exp_new = jnp.exp(score_new)
    denominator = jnp.sum(exp_old, axis=-1, keepdims=True) + jnp.sum(
        exp_new, axis=-1, keepdims=True
    )
    weight_old = (exp_old / denominator).astype(jnp.bfloat16)
    weight_new = (exp_new / denominator).astype(jnp.bfloat16)
    mixed = jnp.einsum(
        "sgmcp,spgd->csgmd", weight_old, values_old, preferred_element_type=jnp.float32
    )
    mixed = mixed + jnp.einsum(
        "sgmcj,jsgd->csgmd", weight_new, values_new, preferred_element_type=jnp.float32
    )
    return mixed.astype(jnp.bfloat16).reshape(span_rows, slot_count, q_width)


def local(
    hidden_rows,
    norm_gain,
    w_query,
    w_key,
    w_value,
    w_out,
    cache_keys,
    cache_values,
    slot_of_request,
    span_length,
    prefix_length,
):
    data_size = lax.axis_size("dp")
    data_index = lax.axis_index("dp")
    per_device = hidden_rows.shape[1]
    q_width = w_query.shape[1]
    kv_width = w_key.shape[1]
    all_requests = slot_of_request.shape[0]
    request_ids = jnp.arange(all_requests, dtype=jnp.int32)
    devices = jnp.arange(data_size, dtype=jnp.int32)
    first_request = data_index * per_device
    my_slots = lax.dynamic_slice_in_dim(slot_of_request, first_request, per_device)
    send_table = (devices[:, None] == my_slots[None, :] // per_device).astype(jnp.bfloat16)
    slot_match = (
        slot_of_request[None, :]
        == (first_request + jnp.arange(per_device, dtype=jnp.int32))[:, None]
    )
    source_match = request_ids[None, :] // per_device == devices[:, None]
    recv_table = jnp.any(slot_match[:, None, :] & source_match[None, :, :], axis=-1).astype(
        jnp.bfloat16
    )
    slot_prefix = jnp.sum(jnp.where(slot_match, prefix_length[None, :], 0), axis=1)
    slot_length = jnp.sum(jnp.where(slot_match, span_length[None, :], 0), axis=1)
    normed = normalize(hidden_rows, norm_gain)
    outgoing = jnp.einsum(
        "js,csf->jcf", send_table, normed, preferred_element_type=jnp.float32
    ).astype(jnp.bfloat16)
    incoming = lax.all_to_all(outgoing, "dp", split_axis=0, concat_axis=0, tiled=True)
    slot_rows = jnp.einsum(
        "sj,jcf->csf", recv_table, incoming, preferred_element_type=jnp.float32
    ).astype(jnp.bfloat16)
    packed = project_group(slot_rows, slot_prefix, w_query, w_key, w_value)
    mixed = attend_slots(
        packed, cache_keys, cache_values, slot_prefix, slot_length, q_width, kv_width
    )
    outgoing_back = jnp.einsum(
        "sj,csf->jcf", recv_table, mixed, preferred_element_type=jnp.float32
    ).astype(jnp.bfloat16)
    returned = lax.all_to_all(outgoing_back, "dp", split_axis=0, concat_axis=0, tiled=True)
    request_heads = jnp.einsum(
        "js,jcf->csf", send_table, returned, preferred_element_type=jnp.float32
    ).astype(jnp.bfloat16)
    span_rows = request_heads.shape[0]
    flat_heads = request_heads.reshape(span_rows * per_device, q_width)
    summed = lax.psum_scatter(
        jnp.dot(flat_heads, w_out, preferred_element_type=jnp.float32).astype(jnp.bfloat16),
        "tensor",
        scatter_dimension=0,
        tiled=True,
    ).astype(jnp.float32)
    return summed.reshape(hidden_rows.shape[0], per_device, -1).astype(jnp.bfloat16)


def solution(mesh):
    placed = (
        P("tensor", "dp", None),
        P(),
        P(None, "tensor"),
        P(None, "tensor"),
        P(None, "tensor"),
        P("tensor", None),
        P("dp", None, "tensor"),
        P("dp", None, "tensor"),
        P(),
        P(),
        P(),
    )
    return jax.shard_map(
        local, mesh=mesh, in_specs=placed, out_specs=P("tensor", "dp", None), check_vma=False
    )
```

profile of v0, /device:TPU:1, one launch (start us, length us, event | category | flops | bytes accessed | tf_op | source)
XLA Modules:
  0.0 441.6 jit_solution(15629852325169047121)
XLA Ops:
  6.5 0.0 copy-start
  6.5 2.6 fusion.16
  9.1 0.7 and_select_fusion
  9.8 7.6 %convolution_convert_fusion.1 = bf16[16,32,8192]{2,0,1:T(8,128)(2,1)} fusion(bf16[32,2,8192]{2,1,0:T(2,128)(2,1)} %param.11, f32[8192]{0:T(1024)} %param.12, f32[32,2]{1,0:T(8,128)S(1)} %add_rsqrt_fusion, s32[2]{0:T(128)S(1)} %and_select_fusion), kind=kOutput, calls=%fused_computation.6 | convolution fusion | flops 23068704 | bytes 9470216 | tf_op jit(solution)/shard_map/js,csf->jcf/dot_general | solution.py:136
  17.5 11.2 %copy.63 = bf16[16,32,8192]{2,1,0:T(8,128)(2,1)} copy(bf16[16,32,8192]{2,0,1:T(8,128)(2,1)} %convolution_convert_fusion.1) | data formatting | bytes 16777216 | tf_op jit(solution)/shard_map/convert_element_type | solution.py:138
  28.7 7.8 %all-to-all-start = ((bf16[16,32,8192]{2,1,0:T(8,128)(2,1)}), bf16[16,32,8192]{2,1,0:T(8,128)(2,1)}, u32[]{:S(2)}, u32[]{:S(2)}) async-start(bf16[16,32,8192]{2,1,0:T(8,128)(2,1)} %copy.63), calls=%async_computation | async-start | bytes 16777216 | tf_op jit(solution)/shard_map/all_to_all | solution.py:139
  36.4 0.2 all-gather.2.cloned.1.call-start
  36.7 0.0 copy-done.4
  36.7 0.0 copy-done.5
  36.7 0.0 copy-done.6
  36.7 0.2 select_reduce_fusion
  36.9 0.1 and_reduce_fusion
  37.0 145.5 %all-to-all-done = bf16[16,32,8192]{2,1,0:T(8,128)(2,1)} async-done(((bf16[16,32,8192]{2,1,0:T(8,128)(2,1)}), bf16[16,32,8192]{2,1,0:T(8,128)(2,1)}, u32[]{:S(2)}, u32[]{:S(2)}) %all-to-all-start) | async-done | bytes 8388640 | tf_op jit(solution)/shard_map/all_to_all | solution.py:139
  182.5 9.4 %fusion.3 = bf16[32,2,8192]{2,1,0:T(2,128)(2,1)} fusion(bf16[16,32,8192]{2,1,0:T(8,128)(2,1)} %all-to-all-done, pred[2,16]{1,0:T(4,128)(4,1)S(1)} %and_reduce_fusion), kind=kOutput, calls=%fused_computation.8 | convolution fusion | flops 17301504 | bytes 9437216 | tf_op jit(solution)/shard_map/sj,jcf->csf/dot_general | solution.py:140
  191.9 0.0 all-gather.2.cloned.1.call-update
  191.9 0.3 reduce-scatter.2.cloned.1.call-start
  192.3 0.1 iota_compare_fusion.3
  192.3 0.1 add_convert_fusion.1
  192.4 0.1 broadcast_and_fusion
  192.5 1.7 multiply_cosine_fusion
  194.3 0.1 iota_compare_fusion.1
  194.4 53.7 %all-gather.2.cloned.1.call-done = bf16[256,2,8192]{2,1,0:T(2,128)(2,1)} async-done(((bf16[32,2,8192]{2,1,0:T(2,128)(2,1)}), bf16[256,2,8192]{2,1,0:T(2,128)(2,1)}) %all-gather.2.cloned.1.call-update) | async-done | bytes 8388624 | tf_op jit(solution)/shard_map/all_gather | solution.py:35
  248.0 8.9 %fusion.38 = f32[256,2,1,128]{0,3,1,2:T(8,128)S(1)} fusion(bf16[8192,128]{1,0:T(8,128)(2,1)} %param.14, bf16[256,2,8192]{2,1,0:T(2,128)(2,1)} %all-gather.2.cloned.1.call-done), kind=kOutput, calls=%fused_computation.38 | convolution fusion | flops 1073741824 | bytes 10747904 | tf_op jit(solution)/shard_map/nsd,df->nsf/dot_general | solution.py:43
  256.9 1.2 fusion.78
  258.1 0.0 copy-done.7
  258.1 13.0 %fusion.6 = f32[256,2,512]{2,0,1:T(8,128)} fusion(bf16[8192,512]{1,0:T(8,128)(2,1)} %param.13, bf16[256,2,8192]{2,1,0:T(2,128)(2,1)S(1)} %copy-done.7), kind=kOutput, calls=%fused_computation.11 | convolution fusion | flops 4294967296 | bytes 17825792 | tf_op jit(solution)/shard_map/nsd,df->nsf/dot_general | solution.py:41
  271.1 1.6 reshape.282
  272.7 0.6 fusion.91
  273.3 1.2 subtract_convert_fusion
  274.5 0.0 copy-start.2
  274.5 0.0 copy-start.3
  274.5 9.1 %fusion.2 = (f32[2,4,256]{2,1,0:T(4,128)S(1)}, f32[2,256,4,2048]{3,1,2,0:T(8,128)}) fusion(pred[2,2048]{1,0:T(4,128)(4,1)S(1)} %iota_compare_fusion.1, bf16[2,2048,128]{2,1,0:T(8,128)(2,1)} %param.17, bf16[256,2,4,64]{3,0,2,1:T(8,128)(2,1)S(1)} %get-tuple-element.9, bf16[256,2,4,64]{3,0,2,1:T(8,128)(2,1)S(1)} %get-tuple-element.8), kind=kOutput, calls=%fused_computation.4 | convolution fusion | flops 1087371264 | bytes 18362368 | tf_op jit(solution)/shard_map/csgmd,spgd->sgmcp/dot_general | solution.py:71
  283.6 0.0 copy-done.3
  283.6 2.1 fusion.22
  285.8 0.0 copy-start.8
  285.8 14.5 %fusion.57 = f32[2,128,4,256]{3,1,2,0:T(8,128)} fusion(f32[2,256,256,4]{2,1,3,0:T(8,128)} %get-tuple-element.19, f32[2,4,256]{2,1,0:T(4,128)S(1)} %add.80, pred[2,256,256]{1,2,0:T(8,128)(4,1)S(1)} %broadcast_and_fusion, bf16[8192,128]{1,0:T(8,128)(2,1)S(1)} %copy-done, bf16[256,2,8192]{2,1,0:T(2,128)(2,1)} %all-gather.2.cloned.1.call-done), kind=kOutput, calls=%fused_computation.44 | convolution fusion | flops 1210122240 | bytes 13770752 | tf_op jit(solution)/shard_map/sgmcj,jsgd->csgmd/dot_general | solution.py:95
  300.3 8.0 %fusion.32 = bf16[2,128,4,256]{3,1,2,0:T(8,128)(2,1)S(1)} fusion(f32[2,128,4,256]{3,1,2,0:T(8,128)} %fusion.57, f32[2,4,256]{2,1,0:T(4,128)S(1)} %add.80, f32[2,256,4,2048]{3,1,2,0:T(8,128)} %get-tuple-element.17, pred[2,2048]{1,0:T(4,128)(4,1)S(1)} %iota_compare_fusion.1, bf16[2,2048,128]{2,1,0:T(8,128)(2,1)S(1)} %copy-done.8), kind=kOutput, calls=%fused_computation.36 | convolution fusion | flops 1091043328 | bytes 19410944 | tf_op jit(solution)/shard_map/sgmcp,spgd->csgmd/dot_general | solution.py:92
  308.3 0.5 copy.75
  308.8 1.6 convolution_convert_fusion.3
  310.5 2.4 copy.76
  312.9 56.0 %all_to_all.10 = bf16[16,256,512]{2,1,0:T(8,128)(2,1)S(1)} all-to-all(bf16[16,256,512]{2,1,0:T(8,128)(2,1)S(1)} %copy.76), channel_id=1, replica_groups=mesh['dp'=16,'tensor'=8] {'dp'}, dimensions={0} | all-to-all | bytes 8388608 | tf_op jit(solution)/shard_map/all_to_all | solution.py:150
  368.8 2.5 fusion.35
  371.4 0.2 reshape.287
  371.6 0.0 copy-start.1
  371.6 10.2 %convolution_convert_fusion = bf16[512,8192]{1,0:T(8,128)(2,1)} fusion(bf16[512,512]{1,0:T(8,128)(2,1)S(1)} %reshape.287, bf16[512,8192]{1,0:T(8,128)(2,1)} %param.16), kind=kOutput, calls=%fused_computation.5 | convolution fusion | flops 4299161600 | bytes 17301504 | tf_op jit(solution)/shard_map/dot_general | solution.py:157
  381.8 0.0 reduce-scatter.2.cloned.1.call-update
  381.8 50.2 %reduce-scatter.2.cloned.1.call-done = bf16[64,8192]{1,0:T(8,128)(2,1)} async-done(((bf16[512,8192]{1,0:T(8,128)(2,1)}), bf16[64,8192]{1,0:T(8,128)(2,1)}) %reduce-scatter.2.cloned.1.call-update) | async-done | bytes 1048592 | tf_op jit(solution)/shard_map/reduce_scatter | solution.py:156
  432.1 2.5 convert_element_type.82
  (15 shorter events, 0.1 us)
Async XLA Ops:
  6.5 279.2 %copy-start = (bf16[8192,128]{1,0:T(8,128)(2,1)S(1)}, bf16[8192,128]{1,0:T(8,128)(2,1)}, u32[]{:S(2)}) copy-start(bf16[8192,128]{1,0:T(8,128)(2,1)} %param.15) | copy-start | bytes 6291460
  28.6 8.0 %copy-start.4 = (s32[32]{0:T(128)S(1)}, s32[32]{0:T(128)}, u32[]{:S(2)}) copy-start(s32[32]{0:T(128)} %param.19) | copy-start | bytes 388
  28.7 8.0 %copy-start.5 = (s32[32]{0:T(128)S(1)}, s32[32]{0:T(128)}, u32[]{:S(2)}) copy-start(s32[32]{0:T(128)} %param.20) | copy-start | bytes 388
  28.7 8.1 %copy-start.6 = (s32[32]{0:T(128)S(1)}, s32[32]{0:T(128)}, u32[]{:S(2)}) copy-start(s32[32]{0:T(128)} %param.21) | copy-start | bytes 388
  28.7 153.8 %all-to-all-start = ((bf16[16,32,8192]{2,1,0:T(8,128)(2,1)}), bf16[16,32,8192]{2,1,0:T(8,128)(2,1)}, u32[]{:S(2)}, u32[]{:S(2)}) async-start(bf16[16,32,8192]{2,1,0:T(8,128)(2,1)} %copy.63), calls=%async_computation | async-start | bytes 16777216 | tf_op jit(solution)/shard_map/all_to_all | solution.py:139
  36.4 211.6 %all-gather.2.cloned.1.call-start = ((), (), s32[]{:S(2)}) async-start(), calls=%async_computation.3 | async-start | bytes 9437184 | tf_op jit(solution)/shard_map/all_gather | solution.py:35
  191.9 240.1 %reduce-scatter.2.cloned.1.call-start = ((), (), s32[]{:S(2)}) async-start(), calls=%async_computation.4 | async-start | bytes 9437184 | tf_op jit(solution)/shard_map/reduce_scatter | solution.py:156
  248.0 10.1 %copy-start.7 = (bf16[256,2,8192]{2,1,0:T(2,128)(2,1)S(1)}, bf16[256,2,8192]{2,1,0:T(2,128)(2,1)}, u32[]{:S(2)}) copy-start(bf16[256,2,8192]{2,1,0:T(2,128)(2,1)} %all-gather.2.cloned.1.call-done) | copy-start | bytes 25165828
  274.5 9.1 %copy-start.2 = (bf16[256,2,64]{0,2,1:T(8,128)(2,1)S(1)}, bf16[256,2,64]{0,2,1:T(8,128)(2,1)}, u32[]{:S(2)}) copy-start(bf16[256,2,64]{0,2,1:T(8,128)(2,1)} %get-tuple-element.12) | copy-start | bytes 196612
  274.5 9.1 %copy-start.3 = (bf16[256,2,64]{0,2,1:T(8,128)(2,1)S(1)}, bf16[256,2,64]{0,2,1:T(8,128)(2,1)}, u32[]{:S(2)}) copy-start(bf16[256,2,64]{0,2,1:T(8,128)(2,1)} %get-tuple-element.13) | copy-start | bytes 196612
  285.8 14.5 %copy-start.8 = (bf16[2,2048,128]{2,1,0:T(8,128)(2,1)S(1)}, bf16[2,2048,128]{2,1,0:T(8,128)(2,1)}, u32[]{:S(2)}) copy-start(bf16[2,2048,128]{2,1,0:T(8,128)(2,1)} %param.18) | copy-start | bytes 3145732
  371.6 63.0 %copy-start.1 = (bf16[8192,128]{1,0:T(8,128)(2,1)S(1)}, bf16[8192,128]{1,0:T(8,128)(2,1)}, u32[]{:S(2)}) copy-start(bf16[8192,128]{1,0:T(8,128)(2,1)} %param.15) | copy-start | bytes 6291460
Sparse Core Ops, SparseCore 0:
  192.1 55.9 all-gather.1
  382.0 50.0 reduce-scatter.1
where the time goes:
time: 448 us; the launch traced here: 442 us
  waiting for transfers between devices  249 us (56%)
  matrix products  87 us (19%)
  blocking collectives  56 us (12%)
  local copies, waits for them, and re-layouts  19 us (4%)
  between operations  13.8 us (3%)
  starting transfers between devices  8.23 us (2%)
  other arithmetic  8.21 us (2%)
    all_to_all x1, waiting for transfers between devices, local(): lax.all_to_all(outgoing, 'dp', split_axis=0, concat_axis=0, tiled=True)  145 us
    all_to_all x1, blocking collectives, local(): lax.all_to_all(outgoing_back, 'dp', split_axis=0, concat_axis=0, tiled=True)  56 us
    all_gather x1, waiting for transfers between devices, project_group(): piece_rows = lax.all_gather(normed, 'tensor', axis=0, tiled=True)  53.7 us
    reduce_scatter x1, waiting for transfers between devices, local(): lax.psum_scatter(jnp.dot(flat_heads, w_out, preferred_element_type=jnp.fl...  50.2 us
    dot_general x1, matrix products, attend_slots(): jnp.einsum('sgmcj,jsgd->csgmd', weight_new, values_new, preferred_element...  14.5 us
    dot_general x1, matrix products, project_group(): jnp.einsum('nsd,df->nsf', piece_rows, w_query, preferred_element_type=jnp...  13 us
    convert_element_type x1, local copies, waits for them, and re-layouts, local(): outgoing = jnp.einsum('js,csf->jcf', send_table, normed, preferred_elemen...  11.2 us
    dot_general x1, matrix products, local(): jnp.dot(flat_heads, w_out, preferred_element_type=jnp.float32)  10.2 us
  transfers between devices with their start and end apart: 3, of which 3 were waited for; matrix products, arithmetic and copies ran while one was open for 1% of the time, Pallas kernels for 0%

commit v1 on v0

--- a/solution.py
+++ b/solution.py
@@ -7,6 +7,17 @@
 rope_base = 500000.0
 norm_eps = 1e-05
 masked = -1e30
+
+
+def around_the_ring(x, axis, d):
+    n_dev = lax.axis_size(axis)
+    route = [(i, (i + 1) % n_dev) for i in range(n_dev)]
+    parts = [x]
+    for stride in range(1, n_dev):
+        parts = [lax.ppermute(parts[0], axis, route), *parts]
+    out = jnp.concatenate(parts, axis=d)
+    shift = (lax.axis_index(axis) + 1) * parts[-1].shape[d]
+    return jnp.roll(out, shift, axis=d)
 
 
 def rotate(values, position):
@@ -32,7 +43,7 @@
 
 
 def project_group(normed, prefix_here, w_query, w_key, w_value):
-    piece_rows = lax.all_gather(normed, "tensor", axis=0, tiled=True)
+    piece_rows = around_the_ring(normed, "tensor", 0)
     row_count = piece_rows.shape[0]
     request_count = piece_rows.shape[1]
     positions = (prefix_here[None, :] + jnp.arange(row_count, dtype=jnp.int32)[:, None]).astype(

time: 448 us -> 537 us (1.20)
  local copies, waits for them, and re-layouts: 19 us -> 59.7 us
  waiting for transfers between devices: 249 us -> 289 us
  starting transfers between devices: 8.23 us -> 27.1 us
  blocking collectives: 56 us -> 47.8 us
    ppermute x0 -> x7, waiting for transfers between devices: none -> 79.8 us  [around_the_ring(): parts = [lax.ppermute(parts[0], axis, route), *parts]]
    all_gather x1 -> x0, waiting for transfers between devices: 53.7 us -> none  [project_group(): piece_rows = lax.all_gather(normed, 'tensor', axis=0, tiled=True)]
    unnamed x18 -> x65, local copies, waits for them, and re-layouts: 0.04 us -> 33.2 us
    ppermute x0 -> x7, starting transfers between devices: none -> 19.1 us  [around_the_ring(): parts = [lax.ppermute(parts[0], axis, route), *parts]]
    reduce_scatter x1, waiting for transfers between devices: 50.2 us -> 64.1 us  [local(): lax.psum_scatter(jnp.dot(flat_heads, w_out, preferred_element_type=jnp.fl...]
    all_to_all x1, blocking collectives: 56 us -> 47.8 us  [local(): lax.all_to_all(outgoing_back, 'dp', split_axis=0, concat_axis=0, tiled=True)]
    dynamic_slice x0 -> x1, local copies, waits for them, and re-layouts: none -> 6.53 us  [around_the_ring(): return jnp.roll(out, shift, axis=d)]
  transfers between devices with their start and end apart: 3 -> 9, of which waited for: 3 -> 9; matrix products, arithmetic and copies ran while one was open for 1% -> 1% of each run, Pallas kernels for 0% -> 0%
where the time goes in v1:
time: 537 us; the launch traced here: 530 us
  waiting for transfers between devices  289 us (54%)
  matrix products  84.7 us (16%)
  local copies, waits for them, and re-layouts  59.7 us (11%)
  blocking collectives  47.8 us (9%)
  starting transfers between devices  27.1 us (5%)
  between operations  14.4 us (3%)
  other arithmetic  6.84 us (1%)
    all_to_all x1, waiting for transfers between devices, local(): lax.all_to_all(outgoing, 'dp', split_axis=0, concat_axis=0, tiled=True)  145 us
    ppermute x7, waiting for transfers between devices, around_the_ring(): parts = [lax.ppermute(parts[0], axis, route), *parts]  79.8 us
    reduce_scatter x1, waiting for transfers between devices, local(): lax.psum_scatter(jnp.dot(flat_heads, w_out, preferred_element_type=jnp.fl...  64.1 us
    all_to_all x1, blocking collectives, local(): lax.all_to_all(outgoing_back, 'dp', split_axis=0, concat_axis=0, tiled=True)  47.8 us
    unnamed x65, local copies, waits for them, and re-layouts  33.2 us
    ppermute x7, starting transfers between devices, around_the_ring(): parts = [lax.ppermute(parts[0], axis, route), *parts]  19.1 us
    dot_general x1, matrix products, attend_slots(): jnp.einsum('sgmcj,jsgd->csgmd', weight_new, values_new, preferred_element...  14.5 us
    dot_general x1, matrix products, project_group(): jnp.einsum('nsd,df->nsf', piece_rows, w_query, preferred_element_type=jnp...  12.9 us
  transfers between devices with their start and end apart: 9, of which 9 were waited for; matrix products, arithmetic and copies ran while one was open for 1% of the time, Pallas kernels for 0%

profile of v1, /device:TPU:1, one launch (start us, length us, event | category | flops | bytes accessed | tf_op | source)
XLA Modules:
  0.0 529.8 jit_solution(2248412847715884853)
XLA Ops:
  6.5 2.6 fusion.16
  10.4 7.6 %convolution_convert_fusion.1 = bf16[16,32,8192]{2,0,1:T(8,128)(2,1)} fusion(bf16[32,2,8192]{2,1,0:T(2,128)(2,1)} %param.11, f32[8192]{0:T(1024)} %param.12, f32[32,2]{1,0:T(8,128)S(1)} %add_rsqrt_fusion, s32[2]{0:T(128)S(1)} %and_select_fusion), kind=kOutput, calls=%fused_computation.6 | convolution fusion | flops 23068704 | bytes 9470216 | tf_op jit(solution)/shard_map/js,csf->jcf/dot_general | solution.py:147
  18.0 11.2 %copy.63 = bf16[16,32,8192]{2,1,0:T(8,128)(2,1)} copy(bf16[16,32,8192]{2,0,1:T(8,128)(2,1)} %convolution_convert_fusion.1) | data formatting | bytes 16777216 | tf_op jit(solution)/shard_map/convert_element_type | solution.py:149
  29.2 7.8 %all-to-all-start = ((bf16[16,32,8192]{2,1,0:T(8,128)(2,1)}), bf16[16,32,8192]{2,1,0:T(8,128)(2,1)}, u32[]{:S(2)}, u32[]{:S(2)}) async-start(bf16[16,32,8192]{2,1,0:T(8,128)(2,1)} %copy.63), calls=%async_computation | async-start | bytes 16777216 | tf_op jit(solution)/shard_map/all_to_all | solution.py:150
  37.6 145.4 %all-to-all-done = bf16[16,32,8192]{2,1,0:T(8,128)(2,1)} async-done(((bf16[16,32,8192]{2,1,0:T(8,128)(2,1)}), bf16[16,32,8192]{2,1,0:T(8,128)(2,1)}, u32[]{:S(2)}, u32[]{:S(2)}) %all-to-all-start) | async-done | bytes 8388640 | tf_op jit(solution)/shard_map/all_to_all | solution.py:150
  183.0 8.5 %fusion.3 = bf16[32,2,8192]{2,1,0:T(2,128)(2,1)S(1)} fusion(bf16[16,32,8192]{2,1,0:T(8,128)(2,1)} %all-to-all-done, pred[2,16]{1,0:T(4,128)(4,1)S(1)} %and_reduce_fusion), kind=kOutput, calls=%fused_computation.8 | convolution fusion | flops 17301504 | bytes 9437216 | tf_op jit(solution)/shard_map/sj,jcf->csf/dot_general | solution.py:151
  191.5 4.1 collective-permute-start
  195.6 11.7 %collective-permute-done = bf16[32,2,8192]{2,1,0:T(2,128)(2,1)S(1)} collective-permute-done((bf16[32,2,8192]{2,1,0:T(2,128)(2,1)S(1)}, bf16[32,2,8192]{2,1,0:T(2,128)(2,1)S(1)}, u32[]{:S(2)}, u32[]{:S(2)}) %collective-permute-start) | collective-permute-done | bytes 1048608 | tf_op jit(solution)/shard_map/ppermute | solution.py:17
  208.3 2.5 collective-permute-start.1
  210.8 11.7 %collective-permute-done.1 = bf16[32,2,8192]{2,1,0:T(2,128)(2,1)S(1)} collective-permute-done((bf16[32,2,8192]{2,1,0:T(2,128)(2,1)S(1)}, bf16[32,2,8192]{2,1,0:T(2,128)(2,1)S(1)}, u32[]{:S(2)}, u32[]{:S(2)}) %collective-permute-start.1) | collective-permute-done | bytes 1048608 | tf_op jit(solution)/shard_map/ppermute | solution.py:17
  223.5 2.5 collective-permute-start.2
  226.0 11.7 %collective-permute-done.2 = bf16[32,2,8192]{2,1,0:T(2,128)(2,1)S(1)} collective-permute-done((bf16[32,2,8192]{2,1,0:T(2,128)(2,1)S(1)}, bf16[32,2,8192]{2,1,0:T(2,128)(2,1)S(1)}, u32[]{:S(2)}, u32[]{:S(2)}) %collective-permute-start.2) | collective-permute-done | bytes 1048608 | tf_op jit(solution)/shard_map/ppermute | solution.py:17
  237.7 1.0 copy-done.7
  238.7 2.5 collective-permute-start.3
  241.2 11.7 %collective-permute-done.3 = bf16[32,2,8192]{2,1,0:T(2,128)(2,1)S(1)} collective-permute-done((bf16[32,2,8192]{2,1,0:T(2,128)(2,1)S(1)}, bf16[32,2,8192]{2,1,0:T(2,128)(2,1)S(1)}, u32[]{:S(2)}, u32[]{:S(2)}) %collective-permute-start.3) | collective-permute-done | bytes 1048608 | tf_op jit(solution)/shard_map/ppermute | solution.py:17
  253.0 1.0 copy-done.9
  253.9 2.5 collective-permute-start.4
  256.4 11.7 %collective-permute-done.4 = bf16[32,2,8192]{2,1,0:T(2,128)(2,1)S(1)} collective-permute-done((bf16[32,2,8192]{2,1,0:T(2,128)(2,1)S(1)}, bf16[32,2,8192]{2,1,0:T(2,128)(2,1)S(1)}, u32[]{:S(2)}, u32[]{:S(2)}) %collective-permute-start.4) | collective-permute-done | bytes 1048608 | tf_op jit(solution)/shard_map/ppermute | solution.py:17
  269.1 2.5 collective-permute-start.5
  271.8 11.6 %collective-permute-done.5 = bf16[32,2,8192]{2,1,0:T(2,128)(2,1)} collective-permute-done((bf16[32,2,8192]{2,1,0:T(2,128)(2,1)S(1)}, bf16[32,2,8192]{2,1,0:T(2,128)(2,1)}, u32[]{:S(2)}, u32[]{:S(2)}) %collective-permute-start.5) | collective-permute-done | bytes 1048608 | tf_op jit(solution)/shard_map/ppermute | solution.py:17
  283.4 2.6 collective-permute-start.6
  286.5 2.0 multiply_cosine_fusion
  288.5 9.5 %collective-permute-done.6 = bf16[32,2,8192]{2,1,0:T(2,128)(2,1)} collective-permute-done((bf16[32,2,8192]{2,1,0:T(2,128)(2,1)}, bf16[32,2,8192]{2,1,0:T(2,128)(2,1)}, u32[]{:S(2)}, u32[]{:S(2)}) %collective-permute-start.6) | collective-permute-done | bytes 1048608 | tf_op jit(solution)/shard_map/ppermute | solution.py:17
  298.0 2.1 constant_dynamic-update-slice_fusion.15
  300.1 2.5 constant_dynamic-update-slice_fusion.14
  302.6 2.6 constant_dynamic-update-slice_fusion.13
  305.3 2.6 constant_dynamic-update-slice_fusion.12
  311.9 2.5 constant_dynamic-update-slice_fusion.7
  314.4 2.5 constant_dynamic-update-slice_fusion.6
  319.0 1.0 constant_dynamic-update-slice_fusion.3
  319.9 1.0 constant_dynamic-update-slice_fusion.2
  320.9 1.4 constant_dynamic-update-slice_fusion.1
  323.3 6.5 %constant_dynamic-slice_fusion = bf16[256,2,8192]{2,1,0:T(2,128)(2,1)S(1)} fusion(bf16[512,2,8192]{2,1,0:T(2,128)(2,1)S(1)} %constant_dynamic-update-slice_fusion, s32[]{:T(128)S(6)} %select_n.53), kind=kLoop, calls=%fused_computation.114 | loop fusion | bytes 16777220 | tf_op jit(solution)/shard_map/jit(_roll_dynamic)/dynamic_slice | solution.py:20
  329.9 3.2 copy-done.2
  333.1 12.9 %fusion.6 = f32[256,2,512]{2,0,1:T(8,128)} fusion(bf16[8192,512]{1,0:T(8,128)(2,1)} %param.13, bf16[256,2,8192]{2,1,0:T(2,128)(2,1)S(1)} %constant_dynamic-slice_fusion), kind=kOutput, calls=%fused_computation.11 | convolution fusion | flops 4294967296 | bytes 17825792 | tf_op jit(solution)/shard_map/nsd,df->nsf/dot_general | solution.py:52
  346.1 1.6 reshape.282
  348.3 8.7 %fusion.38 = f32[256,2,1,128]{0,3,1,2:T(8,128)S(1)} fusion(bf16[8192,128]{1,0:T(8,128)(2,1)} %param.14, bf16[256,2,8192]{2,1,0:T(2,128)(2,1)} %copy-done.2), kind=kOutput, calls=%fused_computation.38 | convolution fusion | flops 1073741824 | bytes 10747904 | tf_op jit(solution)/shard_map/nsd,df->nsf/dot_general | solution.py:54
  357.9 7.8 %fusion.2 = (f32[2,4,256]{2,1,0:T(4,128)S(1)}, f32[2,256,4,2048]{3,1,2,0:T(8,128)}) fusion(pred[2,2048]{1,0:T(4,128)(4,1)S(1)} %iota_compare_fusion.1, bf16[2,2048,128]{2,1,0:T(8,128)(2,1)S(1)} %copy-done.23, bf16[256,2,4,64]{3,0,2,1:T(8,128)(2,1)S(1)} %get-tuple-element.9, bf16[256,2,4,64]{3,0,2,1:T(8,128)(2,1)S(1)} %get-tuple-element.8), kind=kOutput, calls=%fused_computation.4 | convolution fusion | flops 1087371264 | bytes 18362368 | tf_op jit(solution)/shard_map/csgmd,spgd->sgmcp/dot_general | solution.py:82
  365.7 2.2 fusion.22
  367.9 14.5 %fusion.57 = f32[2,128,4,256]{3,1,2,0:T(8,128)} fusion(f32[2,256,256,4]{2,1,3,0:T(8,128)} %get-tuple-element.19, f32[2,4,256]{2,1,0:T(4,128)S(1)} %add.96, pred[2,256,256]{1,2,0:T(8,128)(4,1)S(1)} %broadcast_and_fusion, bf16[8192,128]{1,0:T(8,128)(2,1)S(1)} %copy-done, bf16[256,2,8192]{2,1,0:T(2,128)(2,1)} %copy-done.2), kind=kOutput, calls=%fused_computation.44 | convolution fusion | flops 1210122240 | bytes 13770752 | tf_op jit(solution)/shard_map/sgmcj,jsgd->csgmd/dot_general | solution.py:106
  382.4 8.1 %fusion.32 = bf16[2,128,4,256]{3,1,2,0:T(8,128)(2,1)S(1)} fusion(f32[2,128,4,256]{3,1,2,0:T(8,128)} %fusion.57, f32[2,4,256]{2,1,0:T(4,128)S(1)} %add.96, f32[2,256,4,2048]{3,1,2,0:T(8,128)} %get-tuple-element.17, pred[2,2048]{1,0:T(4,128)(4,1)S(1)} %iota_compare_fusion.1, bf16[2,2048,128]{2,1,0:T(8,128)(2,1)S(1)} %copy-done.24), kind=kOutput, calls=%fused_computation.36 | convolution fusion | flops 1091043328 | bytes 19410944 | tf_op jit(solution)/shard_map/sgmcp,spgd->csgmd/dot_general | solution.py:103
  391.1 1.6 convolution_convert_fusion.3
  392.7 2.4 copy.76
  395.1 47.8 %all_to_all.10 = bf16[16,256,512]{2,1,0:T(8,128)(2,1)S(1)} all-to-all(bf16[16,256,512]{2,1,0:T(8,128)(2,1)S(1)} %copy.76), channel_id=1, replica_groups=mesh['dp'=16,'tensor'=8] {'dp'}, dimensions={0} | all-to-all | bytes 8388608 | tf_op jit(solution)/shard_map/all_to_all | solution.py:161
  442.9 2.5 fusion.35
  445.7 10.3 %convolution_convert_fusion = bf16[512,8192]{1,0:T(8,128)(2,1)} fusion(bf16[512,512]{1,0:T(8,128)(2,1)S(1)} %reshape.287, bf16[512,8192]{1,0:T(8,128)(2,1)} %param.16), kind=kOutput, calls=%fused_computation.5 | convolution fusion | flops 4299161600 | bytes 17301504 | tf_op jit(solution)/shard_map/dot_general | solution.py:168
  455.9 64.1 %reduce-scatter.2.cloned.1.call-done = bf16[64,8192]{1,0:T(8,128)(2,1)} async-done(((bf16[512,8192]{1,0:T(8,128)(2,1)}), bf16[64,8192]{1,0:T(8,128)(2,1)}) %reduce-scatter.2.cloned.1.call-update) | async-done | bytes 1048592 | tf_op jit(solution)/shard_map/reduce_scatter | solution.py:167
  520.0 2.5 convert_element_type.82
  (75 shorter events, 14.5 us)
Async XLA Ops:
  6.5 361.4 %copy-start = (bf16[8192,128]{1,0:T(8,128)(2,1)S(1)}, bf16[8192,128]{1,0:T(8,128)(2,1)}, u32[]{:S(2)}) copy-start(bf16[8192,128]{1,0:T(8,128)(2,1)} %param.15) | copy-start | bytes 6291460
  9.8 0.5 copy-start.18
  29.2 8.1 %copy-start.20 = (s32[32]{0:T(128)S(1)}, s32[32]{0:T(128)}, u32[]{:S(2)}) copy-start(s32[32]{0:T(128)} %param.20) | copy-start | bytes 388
  29.2 8.1 %copy-start.21 = (s32[32]{0:T(128)S(1)}, s32[32]{0:T(128)}, u32[]{:S(2)}) copy-start(s32[32]{0:T(128)} %param.21) | copy-start | bytes 388
  29.2 8.1 %copy-start.22 = (s32[32]{0:T(128)S(1)}, s32[32]{0:T(128)}, u32[]{:S(2)}) copy-start(s32[32]{0:T(128)} %param.19) | copy-start | bytes 388
  29.2 153.8 %all-to-all-start = ((bf16[16,32,8192]{2,1,0:T(8,128)(2,1)}), bf16[16,32,8192]{2,1,0:T(8,128)(2,1)}, u32[]{:S(2)}, u32[]{:S(2)}) async-start(bf16[16,32,8192]{2,1,0:T(8,128)(2,1)} %copy.63), calls=%async_computation | async-start | bytes 16777216 | tf_op jit(solution)/shard_map/all_to_all | solution.py:150
  37.0 483.0 %reduce-scatter.2.cloned.1.call-start = ((), (), s32[]{:S(2)}) async-start(), calls=%async_computation.3 | async-start | bytes 9437184 | tf_op jit(solution)/shard_map/reduce_scatter | solution.py:167
  37.6 153.9 %copy-start.16 = (pred[2,16]{1,0:T(4,128)(4,1)}, pred[2,16]{1,0:T(4,128)(4,1)S(1)}, u32[]{:S(2)}) copy-start(pred[2,16]{1,0:T(4,128)(4,1)S(1)} %and_reduce_fusion) | copy-start | bytes 100
  191.5 15.8 %collective-permute-start = (bf16[32,2,8192]{2,1,0:T(2,128)(2,1)S(1)}, bf16[32,2,8192]{2,1,0:T(2,128)(2,1)S(1)}, u32[]{:S(2)}, u32[]{:S(2)}) collective-permute-start(bf16[32,2,8192]{2,1,0:T(2,128)(2,1)S(1)} %fusion.3), channel_id=1, source_target_pairs={{0,1},{1,2},{2,3},{3,4},{4,5},{5,6},{6,7},{7,0},{8,9},{9,10},{10,1... | collective-permute-start | bytes 3145736 | tf_op jit(solution)/shard_map/ppermute | solution.py:17
  207.4 1.0 copy-start.3
  208.3 14.2 %collective-permute-start.1 = (bf16[32,2,8192]{2,1,0:T(2,128)(2,1)S(1)}, bf16[32,2,8192]{2,1,0:T(2,128)(2,1)S(1)}, u32[]{:S(2)}, u32[]{:S(2)}) collective-permute-start(bf16[32,2,8192]{2,1,0:T(2,128)(2,1)S(1)} %collective-permute-done), channel_id=1, source_target_pairs={{0,1},{1,2},{2,3},{3,4},{4,5},{5,6},{6,7},{7,0},{8,9},{9,10},{10,1... | collective-permute-start | bytes 3145736 | tf_op jit(solution)/shard_map/ppermute | solution.py:17
  222.6 1.0 copy-start.5
  223.5 14.2 %collective-permute-start.2 = (bf16[32,2,8192]{2,1,0:T(2,128)(2,1)S(1)}, bf16[32,2,8192]{2,1,0:T(2,128)(2,1)S(1)}, u32[]{:S(2)}, u32[]{:S(2)}) collective-permute-start(bf16[32,2,8192]{2,1,0:T(2,128)(2,1)S(1)} %collective-permute-done.1), channel_id=1, source_target_pairs={{0,1},{1,2},{2,3},{3,4},{4,5},{5,6},{6,7},{7,0},{8,9},{9,10},{10,1... | collective-permute-start | bytes 3145736 | tf_op jit(solution)/shard_map/ppermute | solution.py:17
  237.7 1.0 copy-start.7
  238.7 14.2 %collective-permute-start.3 = (bf16[32,2,8192]{2,1,0:T(2,128)(2,1)S(1)}, bf16[32,2,8192]{2,1,0:T(2,128)(2,1)S(1)}, u32[]{:S(2)}, u32[]{:S(2)}) collective-permute-start(bf16[32,2,8192]{2,1,0:T(2,128)(2,1)S(1)} %collective-permute-done.2), channel_id=1, source_target_pairs={{0,1},{1,2},{2,3},{3,4},{4,5},{5,6},{6,7},{7,0},{8,9},{9,10},{10,1... | collective-permute-start | bytes 3145736 | tf_op jit(solution)/shard_map/ppermute | solution.py:17
  253.0 1.0 copy-start.9
  253.9 14.2 %collective-permute-start.4 = (bf16[32,2,8192]{2,1,0:T(2,128)(2,1)S(1)}, bf16[32,2,8192]{2,1,0:T(2,128)(2,1)S(1)}, u32[]{:S(2)}, u32[]{:S(2)}) collective-permute-start(bf16[32,2,8192]{2,1,0:T(2,128)(2,1)S(1)} %collective-permute-done.3), channel_id=1, source_target_pairs={{0,1},{1,2},{2,3},{3,4},{4,5},{5,6},{6,7},{7,0},{8,9},{9,10},{10,1... | collective-permute-start | bytes 3145736 | tf_op jit(solution)/shard_map/ppermute | solution.py:17
  268.2 1.0 copy-start.11
  269.1 14.2 %collective-permute-start.5 = (bf16[32,2,8192]{2,1,0:T(2,128)(2,1)S(1)}, bf16[32,2,8192]{2,1,0:T(2,128)(2,1)}, u32[]{:S(2)}, u32[]{:S(2)}) collective-permute-start(bf16[32,2,8192]{2,1,0:T(2,128)(2,1)S(1)} %collective-permute-done.4), channel_id=1, source_target_pairs={{0,1},{1,2},{2,3},{3,4},{4,5},{5,6},{6,7},{7,0},{8,9},{9,10},{10,1... | collective-permute-start | bytes 3145736 | tf_op jit(solution)/shard_map/ppermute | solution.py:17
  283.4 14.6 %collective-permute-start.6 = (bf16[32,2,8192]{2,1,0:T(2,128)(2,1)}, bf16[32,2,8192]{2,1,0:T(2,128)(2,1)}, u32[]{:S(2)}, u32[]{:S(2)}) collective-permute-start(bf16[32,2,8192]{2,1,0:T(2,128)(2,1)} %collective-permute-done.5), channel_id=1, source_target_pairs={{0,1},{1,2},{2,3},{3,4},{4,5},{5,6},{6,7},{7,0},{8,9},{9,10},{10,1... | collective-permute-start | bytes 3145736 | tf_op jit(solution)/shard_map/ppermute | solution.py:17
  286.0 0.5 copy-start.14
  286.0 22.0 %copy-start.8 = (bf16[32,2,8192]{2,1,0:T(2,128)(2,1)S(1)}, bf16[32,2,8192]{2,1,0:T(2,128)(2,1)}, u32[]{:S(2)}) copy-start(bf16[32,2,8192]{2,1,0:T(2,128)(2,1)} %copy-done.7) | copy-start | bytes 3145732
  286.0 22.9 %copy-start.6 = (bf16[32,2,8192]{2,1,0:T(2,128)(2,1)S(1)}, bf16[32,2,8192]{2,1,0:T(2,128)(2,1)}, u32[]{:S(2)}) copy-start(bf16[32,2,8192]{2,1,0:T(2,128)(2,1)} %copy-done.5) | copy-start | bytes 3145732
  286.0 23.9 %copy-start.4 = (bf16[32,2,8192]{2,1,0:T(2,128)(2,1)S(1)}, bf16[32,2,8192]{2,1,0:T(2,128)(2,1)}, u32[]{:S(2)}) copy-start(bf16[32,2,8192]{2,1,0:T(2,128)(2,1)} %copy-done.3) | copy-start | bytes 3145732
  302.6 14.4 %copy-start.12 = (bf16[32,2,8192]{2,1,0:T(2,128)(2,1)S(1)}, bf16[32,2,8192]{2,1,0:T(2,128)(2,1)}, u32[]{:S(2)}) copy-start(bf16[32,2,8192]{2,1,0:T(2,128)(2,1)} %copy-done.11) | copy-start | bytes 3145732
  305.3 12.7 %copy-start.10 = (bf16[32,2,8192]{2,1,0:T(2,128)(2,1)S(1)}, bf16[32,2,8192]{2,1,0:T(2,128)(2,1)}, u32[]{:S(2)}) copy-start(bf16[32,2,8192]{2,1,0:T(2,128)(2,1)} %copy-done.9) | copy-start | bytes 3145732
  329.9 3.3 copy-start.2
  347.6 9.4 %copy-start.15 = (f32[64]{0:T(128)S(1)}, f32[64]{0:T(128)}, u32[]{:S(2)}) copy-start(f32[64]{0:T(128)} %copy-done.14) | copy-start | bytes 772
  347.6 10.0 %copy-start.13 = (f32[256,2,64]{2,0,1:T(8,128)S(1)}, f32[256,2,64]{2,0,1:T(8,128)}, u32[]{:S(2)}) copy-start(f32[256,2,64]{2,0,1:T(8,128)} %get-tuple-element.15) | copy-start | bytes 393220
  348.3 9.7 %copy-start.23 = (bf16[2,2048,128]{2,1,0:T(8,128)(2,1)S(1)}, bf16[2,2048,128]{2,1,0:T(8,128)(2,1)}, u32[]{:S(2)}) copy-start(bf16[2,2048,128]{2,1,0:T(8,128)(2,1)} %param.17) | copy-start | bytes 3145732
  367.9 14.5 %copy-start.24 = (bf16[2,2048,128]{2,1,0:T(8,128)(2,1)S(1)}, bf16[2,2048,128]{2,1,0:T(8,128)(2,1)}, u32[]{:S(2)}) copy-start(bf16[2,2048,128]{2,1,0:T(8,128)(2,1)} %param.18) | copy-start | bytes 3145732
  382.4 8.7 %copy-start.17 = (pred[2,16]{1,0:T(4,128)(4,1)S(1)}, pred[2,16]{1,0:T(4,128)(4,1)}, u32[]{:S(2)}) copy-start(pred[2,16]{1,0:T(4,128)(4,1)} %copy-done.16) | copy-start | bytes 100
  392.7 50.2 %copy-start.19 = (s32[2]{0:T(128)S(1)}, s32[2]{0:T(128)}, u32[]{:S(2)}) copy-start(s32[2]{0:T(128)} %copy-done.18) | copy-start | bytes 28
  445.6 76.9 %copy-start.1 = (bf16[8192,128]{1,0:T(8,128)(2,1)S(1)}, bf16[8192,128]{1,0:T(8,128)(2,1)}, u32[]{:S(2)}) copy-start(bf16[8192,128]{1,0:T(8,128)(2,1)} %param.15) | copy-start | bytes 6291460
Sparse Core Ops, SparseCore 0:
  456.1 63.8 reduce-scatter.1
